TPU v7x, 256 devices: a whole 4x4x8 slice. The times are simulated.
256 devices in a mesh: gx: 64 (over y, x, z_hi, core), gy: 4 (over z_lo).
Axes of the slice: x: 4, y: 4, z: 8 (z_hi: 2, z_lo: 4; z = z_hi * 4 + z_lo), core: 2. Of those that a mesh axis runs over, the one named last changes fastest.
Arguments:
- image: bfloat16 [32, 256, 16, 1024], P(None, 'gx', None, 'gy'), may hold values from -6 to 6
- w_first: bfloat16 [32, 32, 3, 3, 3], replicated, may hold values from -0.21875 to 0.21875
- b_first: float32 [32], replicated, may hold values from -3 to 3
- w_second: bfloat16 [64, 32, 3, 3, 3], replicated, may hold values from -0.21875 to 0.21875
- b_second: float32 [64], replicated, may hold values from -3 to 3
- w_third: bfloat16 [64, 64, 3, 3, 3], replicated, may hold values from -0.15625 to 0.15625
- b_third: float32 [64], replicated, may hold values from -3 to 3
Outputs:
- coarse_out: bfloat16 [64, 128, 8, 512], P(None, 'gx', None, 'gy')
All inputs are finite; a program needn't handle non-finite values.
Results may differ from a plain program's by a relative error of at most 0.0056.
Values may be sent and summed in bfloat16 or wider, within the bound.
A program may use at most 64 MiB of HBM per device.

v0:
```python
import jax
import jax.numpy as jnp
from jax import lax
from jax.sharding import PartitionSpec as P


def extended(cells, sides, width):
    for axis, dim in sides:
        count = lax.axis_size(axis)
        ends = count - 1
        head = lax.slice_in_dim(cells, 0, width, axis=dim)
        tail = lax.slice_in_dim(cells, cells.shape[dim] - width, cells.shape[dim], axis=dim)
        cells = jnp.concatenate(
            [
                lax.ppermute(tail, axis, [(i, (i + 1) % count) for i in range(ends)]),
                cells,
                lax.ppermute(head, axis, [((i + 1) % count, i) for i in range(ends)]),
            ],
            axis=dim,
        )
    return cells


def convolve(padded, kernel, offset):
    summed = lax.conv_general_dilated(
        padded[None],
        kernel,
        (1, 1, 1),
        "VALID",
        dimension_numbers=("NCDHW", "OIDHW", "NCDHW"),
        preferred_element_type=jnp.float32,
    )[0]
    return jnp.maximum(summed + offset[:, None, None, None], 0.0)


def max_pool(values):
    chans, inline, depth, cross = values.shape
    blocks = values.reshape(chans, inline // 2, 2, depth // 2, 2, cross // 2, 2)
    return jnp.max(blocks, axis=(2, 4, 6))


def per_device(image, w_first, b_first, w_second, b_second, w_third, b_third):
    fine_pad = extended(image, (("gx", 1), ("gy", 3)), 1)
    fine_pad = jnp.pad(fine_pad, ((0, 0), (0, 0), (1, 1), (0, 0)))
    layer_one = convolve(fine_pad, w_first, b_first).astype(jnp.bfloat16)
    pooled = max_pool(layer_one)
    padded = extended(pooled, (("gx", 1), ("gy", 3)), 1)
    padded = jnp.pad(padded, ((0, 0), (0, 0), (1, 1), (0, 0)))
    second = convolve(padded, w_second, b_second).astype(jnp.bfloat16)
    padded = extended(second, (("gx", 1), ("gy", 3)), 1)
    padded = jnp.pad(padded, ((0, 0), (0, 0), (1, 1), (0, 0)))
    return convolve(padded, w_third, b_third).astype(jnp.bfloat16)


def solution(mesh):
    placed = (P(None, "gx", None, "gy"), P(), P(), P(), P(), P(), P())
    return jax.shard_map(
        per_device, mesh=mesh, in_specs=placed, out_specs=P(None, "gx", None, "gy"), check_vma=False
    )
```

profile of v0, /device:TPU:24, one launch (start us, length us, event | category | flops | bytes accessed | tf_op | source)
XLA Modules:
  0.0 206.2 jit_solution(7164907930779553973)
XLA Ops:
  3.1 10.9 %collective-permute-start.1 = (bf16[32,1,16,256]{3,2,1,0:T(8,128)(2,1)S(1)}, bf16[32,1,16,256]{3,2,1,0:T(8,128)(2,1)S(1)}, u32[]{:S(2)}, u32[]{:S(2)}) collective-permute-start(bf16[32,1,16,256]{3,2,1,0:T(8,128)(2,1)S(1)} %get-tuple-element.9), channel_id=1, source_target_pairs={{4,0},{8,4},{12,8},{16,12},{20,16},{24,20},{28,24},{32,28},{36,32}... | collective-permute-start | bytes 786440 | tf_op jit(solution)/shard_map/ppermute | solution.py:17
  16.4 5.1 %collective-permute-done.1 = bf16[32,1,16,256]{3,2,1,0:T(8,128)(2,1)S(1)} collective-permute-done((bf16[32,1,16,256]{3,2,1,0:T(8,128)(2,1)S(1)}, bf16[32,1,16,256]{3,2,1,0:T(8,128)(2,1)S(1)}, u32[]{:S(2)}, u32[]{:S(2)}) %collective-permute-start.1) | collective-permute-done | bytes 262176 | tf_op jit(solution)/shard_map/ppermute | solution.py:17
  24.7 3.4 %collective-permute-start.2 = (bf16[32,6,16,1]{0,2,3,1:T(8,128)(2,1)S(1)}, bf16[32,6,16,1]{0,2,3,1:T(8,128)(2,1)S(1)}, u32[]{:S(2)}, u32[]{:S(2)}) collective-permute-start(bf16[32,6,16,1]{0,2,3,1:T(8,128)(2,1)S(1)} %copy.78), channel_id=1, source_target_pairs={{0,1},{1,2},{2,3},{4,5},{5,6},{6,7},{8,9},{9,10},{10,11},{12,13},{... | collective-permute-start | bytes 18440 | tf_op jit(solution)/shard_map/ppermute | solution.py:15
  31.7 3.0 %collective-permute-done.3 = bf16[32,6,16,1]{0,2,3,1:T(8,128)(2,1)S(1)} collective-permute-done((bf16[32,6,16,1]{0,2,3,1:T(8,128)(2,1)S(1)}, bf16[32,6,16,1]{0,2,3,1:T(8,128)(2,1)S(1)}, u32[]{:S(2)}, u32[]{:S(2)}) %collective-permute-start.3) | collective-permute-done | bytes 6176 | tf_op jit(solution)/shard_map/ppermute | solution.py:17
  36.9 5.1 %fusion.17 = bf16[32,6,18,1,258]{4,2,1,0,3:T(8,128)(2,1)S(1)} fusion(bf16[32,6,16,1]{3,2,1,0:T(8,128)(2,1)} %copy.56, bf16[32,6,16,256]{3,2,1,0:T(8,128)(2,1)S(1)} %constant_dynamic-update-slice_fusion, bf16[32,6,16,1]{3,2,1,0:T(8,128)(2,1)S(1)} %copy.55), kind=kLoop, calls=%fused_computation.23 | loop fusion | flops 10699776 | bytes 3368448 | tf_op jit(solution)/shard_map/broadcast_in_dim | solution.py:26
  44.3 10.8 %reshape.41 = bf16[32,6,18,1,8,33]{5,4,2,1,0,3:T(8,128)(2,1)} reshape(bf16[32,6,18,1,264]{4,2,1,0,3:T(8,128)(2,1)} %pad.15) | data formatting | bytes 3649536 | tf_op jit(solution)/shard_map/conv_general_dilated | solution.py:25
  55.2 13.1 %copy.59 = bf16[32,6,18,1,8,33]{0,4,5,2,1,3:T(8,128)(2,1)} copy(bf16[32,6,18,1,8,33]{5,4,2,1,0,3:T(8,128)(2,1)} %reshape.41) | data formatting | bytes 3649536 | tf_op jit(solution)/shard_map/conv_general_dilated | solution.py:25
  69.4 19.3 %broadcast_select_fusion = f32[4,16,8,33,32]{4,2,3,1,0:T(8,128)} fusion(pred[8,33]{0,1:T(8,128)(4,1)S(1)} %copy-done.7, bf16[32,32,3,3,3]{1,0,4,3,2:T(8,128)(2,1)S(1)} %copy-done.5, bf16[32,6,18,1,7,2]{0,4,5,2,1,3:T(8,128)(2,1)S(1)} %slice.56, bf16[32,6,18,1,8,33]{0,4,5,2,1,3:T(8,128)(2,1)} %copy.59), kind=kOutput, calls=%fused_computation.14 | convolution fusion | flops 940627968 | bytes 4139784 | tf_op jit(solution)/shard_map/conv_general_dilated | solution.py:25
  88.7 10.7 %copy.60 = f32[4,16,8,33,32]{3,2,4,1,0:T(8,128)} copy(f32[4,16,8,33,32]{4,2,3,1,0:T(8,128)} %broadcast_select_fusion) | data formatting | bytes 4325376 | tf_op jit(solution)/shard_map/conv_general_dilated | solution.py:25
  99.5 7.4 %reshape.11 = f32[4,16,1,264,32]{3,4,1,0,2:T(8,128)} reshape(f32[4,16,8,33,32]{3,2,4,1,0:T(8,128)} %copy.60) | data formatting | bytes 4325376 | tf_op jit(solution)/shard_map/conv_general_dilated | solution.py:25
  108.7 4.7 %copy.61 = f32[1,32,4,16,256]{1,4,3,2,0:T(8,128)} copy(f32[1,32,4,16,256]{4,1,3,2,0:T(8,128)S(1)} %slice_bitcast_fusion) | data formatting | bytes 4194304 | tf_op jit(solution)/shard_map/conv_general_dilated | solution.py:25
  113.3 10.5 %fusion.10 = bf16[32,2,8,128]{0,3,2,1:T(8,128)(2,1)S(1)} fusion(f32[32,2,2,8,2,128,2]{0,6,5,4,3,2,1:T(2,128)} %bitcast.57, f32[32]{0:T(128)S(1)} %copy-done.2), kind=kLoop, calls=%fused_computation.16 | loop fusion | flops 2031616 | bytes 2228352 | tf_op jit(solution)/shard_map/reduce_max | solution.py:39
  123.9 4.0 %collective-permute-start.4 = (bf16[32,1,8,128]{0,3,2,1:T(8,128)(2,1)S(1)}, bf16[32,1,8,128]{0,3,2,1:T(8,128)(2,1)S(1)}, u32[]{:S(2)}, u32[]{:S(2)}) collective-permute-start(bf16[32,1,8,128]{0,3,2,1:T(8,128)(2,1)S(1)} %get-tuple-element.13), channel_id=1, source_target_pairs={{0,4},{4,8},{8,12},{12,16},{16,20},{20,24},{24,28},{28,32},{32,36}... | collective-permute-start | bytes 196616 | tf_op jit(solution)/shard_map/ppermute | solution.py:15
  127.9 8.5 %collective-permute-start.5 = (bf16[32,1,8,128]{0,3,2,1:T(8,128)(2,1)S(1)}, bf16[32,1,8,128]{0,3,2,1:T(8,128)(2,1)S(1)}, u32[]{:S(2)}, u32[]{:S(2)}) collective-permute-start(bf16[32,1,8,128]{0,3,2,1:T(8,128)(2,1)S(1)} %get-tuple-element.14), channel_id=1, source_target_pairs={{4,0},{8,4},{12,8},{16,12},{20,16},{24,20},{28,24},{32,28},{36,32}... | collective-permute-start | bytes 196616 | tf_op jit(solution)/shard_map/ppermute | solution.py:17
  136.6 7.5 %collective-permute-done.4 = bf16[32,1,8,128]{0,3,2,1:T(8,128)(2,1)S(1)} collective-permute-done((bf16[32,1,8,128]{0,3,2,1:T(8,128)(2,1)S(1)}, bf16[32,1,8,128]{0,3,2,1:T(8,128)(2,1)S(1)}, u32[]{:S(2)}, u32[]{:S(2)}) %collective-permute-start.4) | collective-permute-done | bytes 65568 | tf_op jit(solution)/shard_map/ppermute | solution.py:15
  144.6 3.7 %collective-permute-start.6 = (bf16[32,4,8,1]{3,2,1,0:T(8,128)(2,1)S(1)}, bf16[32,4,8,1]{3,2,1,0:T(8,128)(2,1)S(1)}, u32[]{:S(2)}, u32[]{:S(2)}) collective-permute-start(bf16[32,4,8,1]{3,2,1,0:T(8,128)(2,1)S(1)} %get-tuple-element.15), channel_id=1, source_target_pairs={{0,1},{1,2},{2,3},{4,5},{5,6},{6,7},{8,9},{9,10},{10,11},{12,13},{... | collective-permute-start | bytes 6152 | tf_op jit(solution)/shard_map/ppermute | solution.py:15
  149.6 2.6 %collective-permute-done.6 = bf16[32,4,8,1]{3,2,1,0:T(8,128)(2,1)S(1)} collective-permute-done((bf16[32,4,8,1]{3,2,1,0:T(8,128)(2,1)S(1)}, bf16[32,4,8,1]{3,2,1,0:T(8,128)(2,1)S(1)}, u32[]{:S(2)}, u32[]{:S(2)}) %collective-permute-start.6) | collective-permute-done | bytes 2080 | tf_op jit(solution)/shard_map/ppermute | solution.py:15
  152.1 5.4 %collective-permute-done.7 = bf16[32,4,8,1]{3,2,1,0:T(8,128)(2,1)S(1)} collective-permute-done((bf16[32,4,8,1]{3,2,1,0:T(8,128)(2,1)S(1)}, bf16[32,4,8,1]{3,2,1,0:T(8,128)(2,1)S(1)}, u32[]{:S(2)}, u32[]{:S(2)}) %collective-permute-start.7) | collective-permute-done | bytes 2080 | tf_op jit(solution)/shard_map/ppermute | solution.py:17
  158.6 3.4 %copy.80 = bf16[32,4,10,1,130]{0,1,4,2,3:T(4,128)(2,1)S(1)} copy(bf16[32,4,10,1,130]{4,2,1,0,3:T(8,128)(2,1)S(1)} %fusion.55) | data formatting | bytes 665600
  168.1 10.6 %collective-permute-start.9 = (bf16[64,1,8,128]{0,2,3,1:T(8,128)(2,1)S(1)}, bf16[64,1,8,128]{0,2,3,1:T(8,128)(2,1)S(1)}, u32[]{:S(2)}, u32[]{:S(2)}) collective-permute-start(bf16[64,1,8,128]{0,2,3,1:T(8,128)(2,1)S(1)} %get-tuple-element.12), channel_id=1, source_target_pairs={{4,0},{8,4},{12,8},{16,12},{20,16},{24,20},{28,24},{32,28},{36,32}... | collective-permute-start | bytes 393224 | tf_op jit(solution)/shard_map/ppermute | solution.py:17
  178.7 7.3 %collective-permute-done.8 = bf16[64,1,8,128]{0,2,3,1:T(8,128)(2,1)S(1)} collective-permute-done((bf16[64,1,8,128]{0,2,3,1:T(8,128)(2,1)S(1)}, bf16[64,1,8,128]{0,2,3,1:T(8,128)(2,1)S(1)}, u32[]{:S(2)}, u32[]{:S(2)}) %collective-permute-start.8) | collective-permute-done | bytes 131104 | tf_op jit(solution)/shard_map/ppermute | solution.py:15
  186.0 5.6 %collective-permute-start.10 = (bf16[64,4,8,1]{0,2,3,1:T(8,128)(2,1)S(1)}, bf16[64,4,8,1]{0,2,3,1:T(8,128)(2,1)S(1)}, u32[]{:S(2)}, u32[]{:S(2)}) collective-permute-start(bf16[64,4,8,1]{0,2,3,1:T(8,128)(2,1)S(1)} %get-tuple-element.7), channel_id=1, source_target_pairs={{0,1},{1,2},{2,3},{4,5},{5,6},{6,7},{8,9},{9,10},{10,11},{12,13},{... | collective-permute-start | bytes 12296 | tf_op jit(solution)/shard_map/ppermute | solution.py:15
  193.0 4.2 %collective-permute-done.11 = bf16[64,4,8,1]{0,2,3,1:T(8,128)(2,1)S(1)} collective-permute-done((bf16[64,4,8,1]{0,2,3,1:T(8,128)(2,1)S(1)}, bf16[64,4,8,1]{0,2,3,1:T(8,128)(2,1)S(1)}, u32[]{:S(2)}, u32[]{:S(2)}) %collective-permute-start.11) | collective-permute-done | bytes 4128 | tf_op jit(solution)/shard_map/ppermute | solution.py:17
  200.0 4.3 %fusion.46 = f32[2,8,8,17,64]{4,2,3,1,0:T(8,128)S(1)} fusion(bf16[64,64,3,3,3]{1,0,4,3,2:T(8,128)(2,1)S(1)} %copy-done, bf16[64,4,10,1,7,2]{0,4,5,2,1,3:T(8,128)(2,1)S(1)} %slice.66, bf16[64,4,10,1,8,17]{0,4,5,2,1,3:T(8,128)(2,1)S(1)} %copy.71, pred[8,17]{0,1:T(8,128)(4,1)S(1)} %copy-done.8), kind=kOutput, calls=%fused_computation.53 | convolution fusion | flops 483770368 | bytes 1546376 | tf_op jit(solution)/shard_map/conv_general_dilated | solution.py:25
  (62 shorter events, 34.8 us)
Async XLA Ops:
  0.0 200.0 %copy-start = (bf16[64,64,3,3,3]{1,0,4,3,2:T(8,128)(2,1)S(1)}, bf16[64,64,3,3,3]{1,0,4,3,2:T(8,128)(2,1)}, u32[]{:S(2)}) copy-start(bf16[64,64,3,3,3]{1,0,4,3,2:T(8,128)(2,1)} %param.12) | copy-start | bytes 663556
  0.0 16.3 %copy-start.1 = (bf16[32,4,16,256]{3,2,1,0:T(8,128)(2,1)S(1)}, bf16[32,4,16,256]{3,2,1,0:T(8,128)(2,1)}, u32[]{:S(2)}) copy-start(bf16[32,4,16,256]{3,2,1,0:T(8,128)(2,1)} %param.7) | copy-start | bytes 3145732
  1.2 15.1 %collective-permute-start = (bf16[32,1,16,256]{3,2,1,0:T(8,128)(2,1)S(1)}, bf16[32,1,16,256]{3,2,1,0:T(8,128)(2,1)S(1)}, u32[]{:S(2)}, u32[]{:S(2)}) collective-permute-start(bf16[32,1,16,256]{3,2,1,0:T(8,128)(2,1)S(1)} %get-tuple-element.10), channel_id=1, source_target_pairs={{0,4},{4,8},{8,12},{12,16},{16,20},{20,24},{24,28},{28,32},{32,36}... | collective-permute-start | bytes 786440 | tf_op jit(solution)/shard_map/ppermute | solution.py:15
  3.1 18.3 %collective-permute-start.1 = (bf16[32,1,16,256]{3,2,1,0:T(8,128)(2,1)S(1)}, bf16[32,1,16,256]{3,2,1,0:T(8,128)(2,1)S(1)}, u32[]{:S(2)}, u32[]{:S(2)}) collective-permute-start(bf16[32,1,16,256]{3,2,1,0:T(8,128)(2,1)S(1)} %get-tuple-element.9), channel_id=1, source_target_pairs={{4,0},{8,4},{12,8},{16,12},{20,16},{24,20},{28,24},{32,28},{36,32}... | collective-permute-start | bytes 786440 | tf_op jit(solution)/shard_map/ppermute | solution.py:17
  24.7 5.6 %collective-permute-start.2 = (bf16[32,6,16,1]{0,2,3,1:T(8,128)(2,1)S(1)}, bf16[32,6,16,1]{0,2,3,1:T(8,128)(2,1)S(1)}, u32[]{:S(2)}, u32[]{:S(2)}) collective-permute-start(bf16[32,6,16,1]{0,2,3,1:T(8,128)(2,1)S(1)} %copy.78), channel_id=1, source_target_pairs={{0,1},{1,2},{2,3},{4,5},{5,6},{6,7},{8,9},{9,10},{10,11},{12,13},{... | collective-permute-start | bytes 18440 | tf_op jit(solution)/shard_map/ppermute | solution.py:15
  29.0 5.7 %collective-permute-start.3 = (bf16[32,6,16,1]{0,2,3,1:T(8,128)(2,1)S(1)}, bf16[32,6,16,1]{0,2,3,1:T(8,128)(2,1)S(1)}, u32[]{:S(2)}, u32[]{:S(2)}) collective-permute-start(bf16[32,6,16,1]{0,2,3,1:T(8,128)(2,1)S(1)} %copy.79), channel_id=1, source_target_pairs={{1,0},{2,1},{3,2},{5,4},{6,5},{7,6},{9,8},{10,9},{11,10},{13,12},{... | collective-permute-start | bytes 18440 | tf_op jit(solution)/shard_map/ppermute | solution.py:17
  55.2 14.2 %copy-start.5 = (bf16[32,32,3,3,3]{1,0,4,3,2:T(8,128)(2,1)S(1)}, bf16[32,32,3,3,3]{1,0,4,3,2:T(8,128)(2,1)}, u32[]{:S(2)}) copy-start(bf16[32,32,3,3,3]{1,0,4,3,2:T(8,128)(2,1)} %param.8) | copy-start | bytes 165892
  55.2 14.2 %copy-start.7 = (pred[8,33]{0,1:T(8,128)(4,1)S(1)}, pred[8,33]{0,1:T(8,128)(4,1)}, u32[]{:S(2)}) copy-start(pred[8,33]{0,1:T(8,128)(4,1)} %constant.29) | copy-start | bytes 796
  108.7 4.7 %copy-start.2 = (f32[32]{0:T(128)S(1)}, f32[32]{0:T(128)}, u32[]{:S(2)}) copy-start(f32[32]{0:T(128)} %param.9) | copy-start | bytes 388
  123.9 20.2 %collective-permute-start.4 = (bf16[32,1,8,128]{0,3,2,1:T(8,128)(2,1)S(1)}, bf16[32,1,8,128]{0,3,2,1:T(8,128)(2,1)S(1)}, u32[]{:S(2)}, u32[]{:S(2)}) collective-permute-start(bf16[32,1,8,128]{0,3,2,1:T(8,128)(2,1)S(1)} %get-tuple-element.13), channel_id=1, source_target_pairs={{0,4},{4,8},{8,12},{12,16},{16,20},{20,24},{24,28},{28,32},{32,36}... | collective-permute-start | bytes 196616 | tf_op jit(solution)/shard_map/ppermute | solution.py:15
  127.9 16.3 %collective-permute-start.5 = (bf16[32,1,8,128]{0,3,2,1:T(8,128)(2,1)S(1)}, bf16[32,1,8,128]{0,3,2,1:T(8,128)(2,1)S(1)}, u32[]{:S(2)}, u32[]{:S(2)}) collective-permute-start(bf16[32,1,8,128]{0,3,2,1:T(8,128)(2,1)S(1)} %get-tuple-element.14), channel_id=1, source_target_pairs={{4,0},{8,4},{12,8},{16,12},{20,16},{24,20},{28,24},{32,28},{36,32}... | collective-permute-start | bytes 196616 | tf_op jit(solution)/shard_map/ppermute | solution.py:17
  144.6 7.5 %collective-permute-start.6 = (bf16[32,4,8,1]{3,2,1,0:T(8,128)(2,1)S(1)}, bf16[32,4,8,1]{3,2,1,0:T(8,128)(2,1)S(1)}, u32[]{:S(2)}, u32[]{:S(2)}) collective-permute-start(bf16[32,4,8,1]{3,2,1,0:T(8,128)(2,1)S(1)} %get-tuple-element.15), channel_id=1, source_target_pairs={{0,1},{1,2},{2,3},{4,5},{5,6},{6,7},{8,9},{9,10},{10,11},{12,13},{... | collective-permute-start | bytes 6152 | tf_op jit(solution)/shard_map/ppermute | solution.py:15
  148.3 9.3 %collective-permute-start.7 = (bf16[32,4,8,1]{3,2,1,0:T(8,128)(2,1)S(1)}, bf16[32,4,8,1]{3,2,1,0:T(8,128)(2,1)S(1)}, u32[]{:S(2)}, u32[]{:S(2)}) collective-permute-start(bf16[32,4,8,1]{3,2,1,0:T(8,128)(2,1)S(1)} %get-tuple-element.16), channel_id=1, source_target_pairs={{1,0},{2,1},{3,2},{5,4},{6,5},{7,6},{9,8},{10,9},{11,10},{13,12},{... | collective-permute-start | bytes 6152 | tf_op jit(solution)/shard_map/ppermute | solution.py:17
  162.7 0.9 copy-start.6
  162.7 0.9 copy-start.8
  165.4 0.7 copy-start.3
  166.2 19.8 %collective-permute-start.8 = (bf16[64,1,8,128]{0,2,3,1:T(8,128)(2,1)S(1)}, bf16[64,1,8,128]{0,2,3,1:T(8,128)(2,1)S(1)}, u32[]{:S(2)}, u32[]{:S(2)}) collective-permute-start(bf16[64,1,8,128]{0,2,3,1:T(8,128)(2,1)S(1)} %get-tuple-element.11), channel_id=1, source_target_pairs={{0,4},{4,8},{8,12},{12,16},{16,20},{20,24},{24,28},{28,32},{32,36}... | collective-permute-start | bytes 393224 | tf_op jit(solution)/shard_map/ppermute | solution.py:15
  168.1 17.8 %collective-permute-start.9 = (bf16[64,1,8,128]{0,2,3,1:T(8,128)(2,1)S(1)}, bf16[64,1,8,128]{0,2,3,1:T(8,128)(2,1)S(1)}, u32[]{:S(2)}, u32[]{:S(2)}) collective-permute-start(bf16[64,1,8,128]{0,2,3,1:T(8,128)(2,1)S(1)} %get-tuple-element.12), channel_id=1, source_target_pairs={{4,0},{8,4},{12,8},{16,12},{20,16},{24,20},{28,24},{32,28},{36,32}... | collective-permute-start | bytes 393224 | tf_op jit(solution)/shard_map/ppermute | solution.py:17
  186.0 7.0 %collective-permute-start.10 = (bf16[64,4,8,1]{0,2,3,1:T(8,128)(2,1)S(1)}, bf16[64,4,8,1]{0,2,3,1:T(8,128)(2,1)S(1)}, u32[]{:S(2)}, u32[]{:S(2)}) collective-permute-start(bf16[64,4,8,1]{0,2,3,1:T(8,128)(2,1)S(1)} %get-tuple-element.7), channel_id=1, source_target_pairs={{0,1},{1,2},{2,3},{4,5},{5,6},{6,7},{8,9},{9,10},{10,11},{12,13},{... | collective-permute-start | bytes 12296 | tf_op jit(solution)/shard_map/ppermute | solution.py:15
  191.6 5.5 %collective-permute-start.11 = (bf16[64,4,8,1]{0,2,3,1:T(8,128)(2,1)S(1)}, bf16[64,4,8,1]{0,2,3,1:T(8,128)(2,1)S(1)}, u32[]{:S(2)}, u32[]{:S(2)}) collective-permute-start(bf16[64,4,8,1]{0,2,3,1:T(8,128)(2,1)S(1)} %get-tuple-element.8), channel_id=1, source_target_pairs={{1,0},{2,1},{3,2},{5,4},{6,5},{7,6},{9,8},{10,9},{11,10},{13,12},{... | collective-permute-start | bytes 12296 | tf_op jit(solution)/shard_map/ppermute | solution.py:17
  204.3 0.7 copy-start.4
where the time goes:
time: 208 us; the launch traced here: 206 us
  local copies, waits for them, and re-layouts  70 us (34%)
  starting transfers between devices  54.4 us (26%)
  waiting for transfers between devices  37.2 us (18%)
  matrix products  25.4 us (12%)
  other arithmetic  18.8 us (9%)
    conv_general_dilated x13, local copies, waits for them, and re-layouts, convolve(): lax.conv_general_dilated(padded[None], kernel, (1, 1, 1), 'VALID', dimens...  50.7 us
    ppermute x6, starting transfers between devices, extended(): lax.ppermute(head, axis, [((i + 1) % count, i) for i in range(ends)])  33.8 us
    conv_general_dilated x3, matrix products, convolve(): lax.conv_general_dilated(padded[None], kernel, (1, 1, 1), 'VALID', dimens...  25.4 us
    ppermute x6, starting transfers between devices, extended(): lax.ppermute(tail, axis, [(i, (i + 1) % count) for i in range(ends)])  20.5 us
    ppermute x6, waiting for transfers between devices, extended(): lax.ppermute(tail, axis, [(i, (i + 1) % count) for i in range(ends)])  19.5 us
    ppermute x6, waiting for transfers between devices, extended(): lax.ppermute(head, axis, [((i + 1) % count, i) for i in range(ends)])  17.7 us
    reduce_max x1, other arithmetic, max_pool(): return jnp.max(blocks, axis=(2, 4, 6))  10.5 us
    broadcast_in_dim x3, other arithmetic, convolve(): padded[None]  8.01 us
  transfers between devices with their start and end apart: 12, of which 8 were waited for; matrix products, arithmetic and copies ran while one was open for 1% of the time, Pallas kernels for 0%

commit v1 on v0

v1 whole, which is shorter than its diff:
```python
import functools

import jax
import jax.numpy as jnp
from jax import lax
from jax.experimental import pallas as pl
from jax.experimental.pallas import tpu as pltpu
from jax.sharding import PartitionSpec as P

BF = jnp.bfloat16
F32 = jnp.float32
MESH = pl.DeviceIdType.MESH

FINE = ((0, -1), (0, 1), (-1, -1), (-1, 1), (1, -1), (1, 1))
COARSE = ((0, -1), (0, 1), (-1, 0), (-1, -1), (-1, 1), (1, 0), (1, -1), (1, 1))


def slot_of(dx, dy):
    order = {0: 0, -1: 1, 1: 2}
    return 3 * order[dx] + order[dy]


def iota(shape, dim):
    return lax.broadcasted_iota(jnp.int32, shape, dim)


def onehot(cond):
    return jnp.where(cond, 1.0, 0.0).astype(BF)


def mm(a, b):
    return jnp.dot(a, b, preferred_element_type=F32)


def mm_tn(a, b):
    return lax.dot_general(a, b, (((0,), (0,)), ((), ())), preferred_element_type=F32)


def mm_nt(a, b):
    return lax.dot_general(a, b, (((1,), (1,)), ((), ())), preferred_element_type=F32)


def build_banded(u_ref, t_ref, chans, lanes, depth, parities):
    row = iota((8, 128), 0)
    z_in = iota((8, 128), 1) % depth

    def tap(k, carry):
        a, f = k // 3, k % 3
        for par in range(parities):
            masks = [z_in == parities * row + par + e - 1 for e in range(3)]
            for pair in range(chans // 2):
                for lt in range(lanes // 128):
                    halves = []
                    for o in (2 * pair, 2 * pair + 1):
                        value = jnp.zeros((8, 128), F32)
                        for e in range(3):
                            line = u_ref[(a * 3 + e) * 3 + f, o:o + 1, lt * 128:(lt + 1) * 128]
                            value = jnp.where(masks[e], jnp.broadcast_to(line, (8, 128)), value)
                        halves.append(value)
                    block = jnp.concatenate(halves, axis=0).astype(BF)
                    top = par * chans * 8 + pair * 16
                    t_ref[top:top + 16, pl.ds(pl.multiple_of(k * lanes + lt * 128, 128), 128)] = block
        return carry

    lax.fori_loop(0, 9, tap, 0)


def kernel(nx, ny, image, w1, b1, w2, b2, w3, b3, out,
           x_v, w1_v, w2_v, w3_v, u1, u2, u3, t1, t2, t3, bb, acc, split, fine_pk, own_pk,
           sel, p_own, p_left, p_right, coarse_pk, own_pk2, p3, s_v, s3, bias1, bias2, bias3,
           local_sems, send_x, recv_x, send_f, recv_f, send_p, recv_p, send_c, recv_c):
    gx, gy = lax.axis_index("gx"), lax.axis_index("gy")

    def at(dx, dy):
        return (lax.rem(gx + dx + nx, nx), lax.rem(gy + dy + ny, ny))

    first_x, last_x = gx == 0, gx == nx - 1
    first_y, last_y = gy == 0, gy == ny - 1

    loads = [pltpu.make_async_copy(image.at[:, r], x_v.at[r + 1], local_sems.at[r]) for r in range(4)]
    loads += [pltpu.make_async_copy(src, dst, local_sems.at[4 + i])
              for i, (src, dst) in enumerate(((w1, w1_v), (w2, w2_v), (w3, w3_v)))]
    for load in loads:
        load.start()

    barrier = pltpu.get_barrier_semaphore()
    for d in COARSE:
        pl.semaphore_signal(barrier, inc=1, device_id=at(*d), device_id_type=MESH)

    for load in loads[:4]:
        load.wait()
    ends = jnp.zeros((16, 512), F32)
    r16, l16 = iota((16, 256), 0), iota((16, 256), 1)
    for r in range(4):
        pick = onehot(((r16 == 2 * r) & (l16 == 0)) | ((r16 == 2 * r + 1) & (l16 == 255)))
        ends = ends + mm_nt(pick, x_v[r + 1].reshape(512, 256))
    own_pk[...] = ends.astype(BF)

    pl.semaphore_wait(barrier, len(COARSE))

    rows_x = []
    for i, (r, dst, dx) in enumerate(((0, 5, -1), (3, 0, 1))):
        rows_x.append(pltpu.make_async_remote_copy(
            src_ref=image.at[:, r], dst_ref=x_v.at[dst], send_sem=send_x.at[i], recv_sem=recv_x.at[i],
            device_id=at(dx, 0), device_id_type=MESH))
    for copy in rows_x:
        copy.start()
    fine = {}
    for i, d in enumerate(FINE):
        back = FINE.index((-d[0], -d[1]))
        fine[d] = pltpu.make_async_remote_copy(
            src_ref=own_pk, dst_ref=fine_pk.at[back], send_sem=send_f.at[i], recv_sem=recv_f.at[back],
            device_id=at(*d), device_id_type=MESH)
        fine[d].start()

    for k, (src, dst, n) in enumerate(((b1, bias1, 32), (b2, bias2, 64), (b3, bias3, 64))):
        for o in range(n):
            dst[o * 8:(o + 1) * 8, :] = jnp.full((8, 128), src[o], F32)

    for load in loads[4:]:
        load.wait()
    q1 = onehot(iota((32, 512), 1) // 16 == iota((32, 512), 0))
    u1[...] = mm(w1_v[...].reshape(864, 32), q1).reshape(27, 32, 512)
    build_banded(u1, t1, 32, 512, 16, 2)

    sy, sl = iota((256, 512), 0), iota((256, 512), 1)
    part, pos = sl // 128, sl % 128
    split[...] = onehot(sy == 2 * pos + part - 1)

    def stack_row(i, pack, left, right, keep):
        d = mm(x_v[i].reshape(512, 256), split[...])
        r32, l32 = iota((32, 256), 0), iota((32, 256), 1)
        pick = onehot(((r32 == left) & (l32 == 0)) | ((r32 == right) & (l32 == 255)))
        h = mm_tn(pack, pick)
        odd_before = d[:, :128] + h[:, :128]
        even_after = d[:, 384:] + h[:, 128:]
        full = jnp.concatenate([odd_before, d[:, 128:384], even_after], axis=1)
        if keep is not None:
            full = full * keep
        full = full.astype(BF)
        for f in range(3):
            start = i * 1536 + f * 512
            if not isinstance(start, int):
                start = pl.multiple_of(start, 512)
            bb[pl.ds(start, 512), :] = full[:, f * 128:f * 128 + 256]

    fine[(0, 1)].wait_recv()
    fine[(0, -1)].wait_recv()

    def own_row(i, carry):
        left = jnp.where(first_y, -1, 2 * (i - 1) + 1)
        right = jnp.where(last_y, -1, 16 + 2 * (i - 1))
        stack_row(i, fine_pk[0:2].reshape(32, 512), left, right, None)
        return carry

    lax.fori_loop(1, 5, own_row, 0)

    acc[0] = mm(t1[:, 1536:], bb[1536:4608, :])

    def middle(i, carry):
        acc[i] = mm(t1[...], bb[pl.ds(pl.multiple_of(i * 1536, 512), 4608), :])
        return carry

    lax.fori_loop(1, 3, middle, 0)
    acc[3] = mm(t1[:, :3072], bb[4608:7680, :])

    for tap in range(27):
        q2 = onehot(iota((32, 256), 1) // 8 == iota((32, 256), 0))
        u2[tap] = mm_tn(w2_v[tap], q2)
    build_banded(u2, t2, 64, 256, 8, 1)
    q3 = onehot(iota((64, 512), 1) // 8 == iota((64, 512), 0))
    u3[...] = mm(w3_v[...].reshape(1728, 64), q3).reshape(27, 64, 512)
    build_banded(u3, t3, 64, 512, 8, 1)

    r144 = iota((144, 256), 0)
    l144 = iota((144, 256), 1)
    for jj in range(6):
        dx, j = ((-1, 0, 1)[jj // 2], jj % 2)
        left = slot_of(dx, -1) * 16 + j * 4 + 3
        right = slot_of(dx, 1) * 16 + j * 4
        sel[:, jj * 256:(jj + 1) * 256] = onehot(
            ((r144 == left) & (l144 == 0)) | ((r144 == right) & (l144 == 255)))
    re, le = iota((144, 128), 0), iota((144, 128), 1)
    xo, side = le // 2, le % 2
    for a in range(3):
        jj = xo + a
        group = jnp.where(jj < 2, 1, jnp.where(jj < 4, 0, 2))
        for f in range(3):
            dyl, cil = ((1, 2), (1, 3), (0, 0))[f]
            dyr, cir = ((0, 3), (2, 0), (2, 1))[f]
            want = jnp.where(side == 0, dyl * 16 + cil, dyr * 16 + cir) + group * 48 + (jj % 2) * 4
            tile = 1536 + (a * 3 + f) * 128
            sel[:, tile:tile + 128] = onehot((re == want) & (le < 8))

    def from_side(i, dx, copy):
        copy.wait_recv()
        fine[(-dx, 1)].wait_recv()
        fine[(-dx, -1)].wait_recv()
        edge = first_x if dx < 0 else last_x
        r = 3 if dx < 0 else 0
        left = jnp.where(first_y, -1, 2 * r + 1)
        right = jnp.where(last_y, -1, 16 + 2 * r)
        base = 2 if dx < 0 else 4
        stack_row(i, fine_pk[base:base + 2].reshape(32, 512), left, right, jnp.where(edge, 0.0, 1.0))

    def pool(x):
        m = jnp.maximum(acc[2 * x], acc[2 * x + 1])
        m = jnp.maximum(m[:, :128], m[:, 128:])
        m = jnp.maximum(m[:256], m[256:])
        p_own[x] = jnp.maximum(m + bias1[...], 0.0).astype(BF)

    from_side(0, -1, rows_x[1])
    acc[0] += mm(t1[:, :1536], bb[0:1536, :])
    pool(0)
    from_side(5, 1, rows_x[0])
    acc[3] += mm(t1[:, 3072:], bb[7680:9216, :])
    pool(1)

    rows_p = []
    for i, (dst, dx) in enumerate(((p_right, -1), (p_left, 1))):
        rows_p.append(pltpu.make_async_remote_copy(
            src_ref=p_own, dst_ref=dst, send_sem=send_p.at[i], recv_sem=recv_p.at[i],
            device_id=at(dx, 0), device_id_type=MESH))
    for copy in rows_p:
        copy.start()
    ends = jnp.zeros((16, 256), F32)
    r16, l16 = iota((16, 128), 0), iota((16, 128), 1)
    for j in range(2):
        pick = onehot((r16 // 4 == j) & (l16 == jnp.where(r16 % 4 < 2, r16 % 4, 124 + r16 % 4)))
        ends = ends + mm_nt(pick, p_own[j])
    own_pk2[...] = ends.astype(BF)
    coarse = {}
    for i, d in enumerate(COARSE):
        back = COARSE.index((-d[0], -d[1]))
        coarse[d] = pltpu.make_async_remote_copy(
            src_ref=own_pk2, dst_ref=coarse_pk.at[slot_of(-d[0], -d[1])], send_sem=send_c.at[i],
            recv_sem=recv_c.at[back], device_id=at(*d), device_id_type=MESH)
        coarse[d].start()
    coarse_pk[0] = ends.astype(BF)

    for copy in coarse.values():
        copy.wait_recv()
    rr = iota((144, 256), 0) // 16
    gone_x = ((rr // 3 == 1) & first_x) | ((rr // 3 == 2) & last_x)
    gone_y = ((rr % 3 == 1) & first_y) | ((rr % 3 == 2) & last_y)
    packs = coarse_pk[...].reshape(144, 256)
    packs = jnp.where(gone_x | gone_y, 0.0, packs.astype(F32)).astype(BF)
    h = mm_tn(packs, sel[...])
    for k in range(9):
        p3[k * 256:(k + 1) * 256, 512:640] = h[:, 1536 + k * 128:1664 + k * 128].astype(BF)

    ys, js = iota((128, 256), 0), iota((128, 256), 1)
    shift = onehot(ys == jnp.where(js < 128, js - 1, js - 127))

    def place(jj, p):
        g = (mm(p, shift) + h[:, jj * 256:(jj + 1) * 256]).astype(BF)
        parts = (g[:, :128], p, g[:, 128:])
        for a in range(3):
            if 0 <= jj - a < 4:
                for f in range(3):
                    top = (a * 3 + f) * 256
                    p3[top:top + 256, (jj - a) * 128:(jj - a + 1) * 128] = parts[f]

    place(2, p_own[0])
    place(3, p_own[1])
    for copy, src, base, edge in ((rows_p[1], p_left, 0, first_x), (rows_p[0], p_right, 4, last_x)):
        copy.wait_recv()
        keep = jnp.where(edge, 0.0, 1.0)
        for j in range(2):
            place(base + j, (src[j].astype(F32) * keep).astype(BF))

    lane = iota((1, 640), 1)
    tile, low = lane // 128, lane % 128
    row = jnp.where(tile < 4, tile, low // 2)
    gone = ((row == 0) & first_x) | ((row == 3) & last_x)
    gone = gone | ((tile == 4) & (((low % 2 == 0) & first_y) | ((low % 2 == 1) & last_y)))
    keep = jnp.where(gone, 0.0, 1.0)
    s = mm(t2[...], p3[...])
    s = jnp.maximum(s + jnp.concatenate([bias2[...]] * 5, axis=1), 0.0) * keep
    s_v[...] = s.astype(BF)

    ye, je = iota((128, 256), 0), iota((128, 256), 1)
    for x in range(4):
        mid = s_v[:, x * 128:(x + 1) * 128]
        pick = onehot(((ye == 2 * x) & (je == 0)) | ((ye == 2 * x + 1) & (je == 255)))
        both = jnp.concatenate([mid, s_v[:, 512:640]], axis=1)
        g = mm(both, jnp.concatenate([shift, pick], axis=0)).astype(BF)
        parts = (g[:, :128], mid, g[:, 128:])
        for a in range(3):
            if 0 <= x - a < 2:
                for f in range(3):
                    top = (a * 3 + f) * 512
                    s3[top:top + 512, (x - a) * 128:(x - a + 1) * 128] = parts[f]

    c = mm(t3[...], s3[...])
    c = jnp.maximum(c + jnp.concatenate([bias3[...]] * 2, axis=1), 0.0)
    for x in range(2):
        out[:, x] = c[:, x * 128:(x + 1) * 128].reshape(64, 8, 128).astype(BF)

    for copy in rows_x + list(fine.values()) + rows_p + list(coarse.values()):
        copy.wait_send()


def per_device(image, w_first, b_first, w_second, b_second, w_third, b_third):
    nx, ny = lax.axis_size("gx"), lax.axis_size("gy")
    w1 = jnp.transpose(w_first, (2, 3, 4, 0, 1)).reshape(27, 32, 32)
    w2 = jnp.transpose(w_second, (2, 3, 4, 1, 0)).reshape(27, 32, 64)
    w3 = jnp.transpose(w_third, (2, 3, 4, 0, 1)).reshape(27, 64, 64)
    anywhere = pl.BlockSpec(memory_space=pl.ANY)
    scalars = pl.BlockSpec(memory_space=pltpu.SMEM)
    dma = pltpu.SemaphoreType.DMA
    return pl.pallas_call(
        functools.partial(kernel, nx, ny),
        out_shape=jax.ShapeDtypeStruct((64, 2, 8, 128), BF),
        in_specs=[anywhere, anywhere, scalars, anywhere, scalars, anywhere, scalars],
        out_specs=pl.BlockSpec(memory_space=pltpu.VMEM),
        scratch_shapes=[
            pltpu.VMEM((6, 32, 16, 256), BF),
            pltpu.VMEM((27, 32, 32), BF),
            pltpu.VMEM((27, 32, 64), BF),
            pltpu.VMEM((27, 64, 64), BF),
            pltpu.VMEM((27, 32, 512), F32),
            pltpu.VMEM((27, 64, 256), F32),
            pltpu.VMEM((27, 64, 512), F32),
            pltpu.VMEM((512, 4608), BF),
            pltpu.VMEM((512, 2304), BF),
            pltpu.VMEM((512, 4608), BF),
            pltpu.VMEM((9216, 256), BF),
            pltpu.VMEM((4, 512, 256), F32),
            pltpu.VMEM((256, 512), BF),
            pltpu.VMEM((6, 16, 512), BF),
            pltpu.VMEM((16, 512), BF),
            pltpu.VMEM((144, 2688), BF),
            pltpu.VMEM((2, 256, 128), BF),
            pltpu.VMEM((2, 256, 128), BF),
            pltpu.VMEM((2, 256, 128), BF),
            pltpu.VMEM((9, 16, 256), BF),
            pltpu.VMEM((16, 256), BF),
            pltpu.VMEM((2304, 640), BF),
            pltpu.VMEM((512, 640), BF),
            pltpu.VMEM((4608, 256), BF),
            pltpu.VMEM((256, 128), F32),
            pltpu.VMEM((512, 128), F32),
            pltpu.VMEM((512, 128), F32),
            dma((7,)), dma((2,)), dma((2,)), dma((6,)), dma((6,)),
            dma((2,)), dma((2,)), dma((8,)), dma((8,)),
        ],
        compiler_params=pltpu.CompilerParams(
            collective_id=0, has_side_effects=True, vmem_limit_bytes=60 * 1024 * 1024),
        name="encoder",
    )(image, w1, b_first, w2, b_second, w3, b_third)


def solution(mesh):
    placed = (P(None, "gx", None, "gy"), P(), P(), P(), P(), P(), P())
    return jax.shard_map(
        per_device, mesh=mesh, in_specs=placed, out_specs=P(None, "gx", None, "gy"), check_vma=False
    )
```

time: 208 us -> 58.8 us (0.28)
  the two profiles are of different devices: /device:TPU:24 before, /device:TPU:8 now
where the time goes in v1:
time: 58.8 us; the launch traced here: 58.7 us
  Pallas kernels  57 us (97%)
  local copies, waits for them, and re-layouts  1.67 us (3%)
    pallas_call x1, Pallas kernels, per_device(): pl.pallas_call(functools.partial(kernel, nx, ny), out_shape=jax.ShapeDtyp...  57 us
    unnamed x1, local copies, waits for them, and re-layouts  1.67 us

profile of v1, /device:TPU:8, one launch (start us, length us, event | category | flops | bytes accessed | tf_op | source)
XLA Modules:
  0.0 58.7 jit_solution(17296558998478773450)
XLA Ops:
  0.0 57.0 %encoder.1 = bf16[64,2,8,128]{3,2,1,0:T(8,128)(2,1)} custom-call(bf16[32,4,16,256]{3,2,1,0:T(8,128)(2,1)} %image.1, bf16[27,32,32]{2,1,0:T(8,128)(2,1)} %bitcast.10, f32[32]{0:T(128)} %b1.1, bf16[27,32,64]{2,1,0:T(8,128)(2,1)} %bitcast.11, f32[64]{0:T(128)} %b2.1, bf16[27,64,64]{2,1,0:T(8,128)(2,1)} %bitcast.9, f32[64]{0:T(128)} %b3.1), custom_call_target="tpu_custom_call" | custom-call | tf_op jit(solution)/shard_map/encoder/pallas_call | solution.py:312
  57.0 1.7 %copy.9 = bf16[64,2,8,128]{3,2,1,0:T(8,128)(2,1)} copy(bf16[64,2,8,128]{3,2,1,0:T(8,128)(2,1)} %encoder.1) | data formatting | bytes 524288

commit v2 on v1

v2 whole, which is shorter than its diff:
```python
import functools

import jax
import jax.numpy as jnp
from jax import lax
from jax.experimental import pallas as pl
from jax.experimental.pallas import tpu as pltpu
from jax.sharding import PartitionSpec as P

BF = jnp.bfloat16
F32 = jnp.float32
MESH = pl.DeviceIdType.MESH

FINE = ((0, -1), (0, 1), (-1, -1), (-1, 1), (1, -1), (1, 1))
COARSE = ((0, -1), (0, 1), (-1, 0), (-1, -1), (-1, 1), (1, 0), (1, -1), (1, 1))


def slot_of(dx, dy):
    order = {0: 0, -1: 1, 1: 2}
    return 3 * order[dx] + order[dy]


def iota(shape, dim):
    return lax.broadcasted_iota(jnp.int32, shape, dim)


def onehot(cond):
    return jnp.where(cond, 1.0, 0.0).astype(BF)


def mm(a, b):
    return jnp.dot(a, b, preferred_element_type=F32)


def mm_tn(a, b):
    return lax.dot_general(a, b, (((0,), (0,)), ((), ())), preferred_element_type=F32)


def mm_nt(a, b):
    return lax.dot_general(a, b, (((1,), (1,)), ((), ())), preferred_element_type=F32)


def build_banded(u_ref, t_ref, chans, lanes, depth, parities, groups):
    row = iota((8, 128), 0)
    z_in = iota((8, 128), 1) % depth

    def tap(k, carry):
        a, f = k // 3, k % 3
        for par in range(parities):
            masks = [z_in == parities * row + par + e - 1 for e in range(3)]
            for pair in range(chans // 2):
                for lt in range(lanes // 128):
                    halves = []
                    for o in (2 * pair, 2 * pair + 1):
                        value = jnp.zeros((8, 128), F32)
                        for e in range(3):
                            line = u_ref[(a * 3 + e) * 3 + f, o:o + 1, lt * 128:(lt + 1) * 128]
                            value = jnp.where(masks[e], jnp.broadcast_to(line, (8, 128)), value)
                        halves.append(value)
                    block = jnp.concatenate(halves, axis=0).astype(BF)
                    top = par * chans * 8 + pair * 16
                    part = lanes // groups
                    group, rest = lt * 128 // part, lt * 128 % part
                    lane = a * (3 * lanes) + f * part + (group * 3 * part + rest)
                    t_ref[top:top + 16, pl.ds(pl.multiple_of(lane, 128), 128)] = block
        return carry

    lax.fori_loop(0, 9, tap, 0)


def kernel(nx, ny, image, w1, b1, w2, b2, w3, b3, out,
           x_v, w1_v, w2_v, w3_v, u1, u2, u3, t1, t2, t3, bb, acc, split, shift, fine_pk, own_pk,
           sel, p_own, p_left, p_right, coarse_pk, own_pk2, p_mid, p_lo, p_hi, p_mix, p_edge, s_acc, s_v, s3,
           bias1, bias2, bias3, b1_s, b2_s, b3_s,
           local_sems, send_x, recv_x, send_f, recv_f, send_p, recv_p, send_c, recv_c):
    gx, gy = lax.axis_index("gx"), lax.axis_index("gy")

    def at(dx, dy):
        return (lax.rem(gx + dx + nx, nx), lax.rem(gy + dy + ny, ny))

    first_x, last_x = gx == 0, gx == nx - 1
    first_y, last_y = gy == 0, gy == ny - 1

    barrier = pltpu.get_barrier_semaphore()
    for d in COARSE:
        pl.semaphore_signal(barrier, inc=1, device_id=at(*d), device_id_type=MESH)

    loads = [pltpu.make_async_copy(w1, w1_v, local_sems.at[0])]
    loads += [pltpu.make_async_copy(image.at[:, r], x_v.at[r + 1], local_sems.at[r + 1]) for r in range(4)]
    loads += [pltpu.make_async_copy(src, dst, local_sems.at[5 + i]) for i, (src, dst) in enumerate(
        ((w2, w2_v), (w3, w3_v), (b1, b1_s), (b2, b2_s), (b3, b3_s)))]
    for load in loads:
        load.start()

    loads[0].wait()
    q1 = onehot(iota((32, 512), 1) // 16 == iota((32, 512), 0))
    u1[...] = mm(w1_v[...].reshape(864, 32), q1).reshape(27, 32, 512)
    build_banded(u1, t1, 32, 512, 16, 2, 2)

    for load in loads[1:5]:
        load.wait()
    ends = jnp.zeros((16, 512), F32)
    r16, l16 = iota((16, 256), 0), iota((16, 256), 1)
    for r in range(4):
        pick = onehot(((r16 == 2 * r) & (l16 == 0)) | ((r16 == 2 * r + 1) & (l16 == 255)))
        ends = ends + mm_nt(pick, x_v[r + 1].reshape(512, 256))
    own_pk[...] = ends.astype(BF)

    pl.semaphore_wait(barrier, len(COARSE))

    fine = {}
    for i, d in enumerate(FINE):
        back = FINE.index((-d[0], -d[1]))
        fine[d] = pltpu.make_async_remote_copy(
            src_ref=own_pk, dst_ref=fine_pk.at[back], send_sem=send_f.at[i], recv_sem=recv_f.at[back],
            device_id=at(*d), device_id_type=MESH)
        fine[d].start()

    def row_copy(i, h):
        r, dst, dx = ((0, 5, -1), (3, 0, 1))[i]
        chans = pl.ds(h * 16, 16)
        return pltpu.make_async_remote_copy(
            src_ref=image.at[chans, r], dst_ref=x_v.at[dst, chans], send_sem=send_x.at[i, h],
            recv_sem=recv_x.at[i, h], device_id=at(dx, 0), device_id_type=MESH)

    for h in range(2):
        for i in range(2):
            row_copy(i, h).start()

    for load in loads[5:]:
        load.wait()
    for src, dst, n in ((b1_s, bias1, 32), (b2_s, bias2, 64), (b3_s, bias3, 64)):
        for o in range(n):
            dst[o * 8:(o + 1) * 8, :] = jnp.full((8, 128), src[o], F32)

    q2 = onehot(iota((32, 256), 1) // 8 == iota((32, 256), 0))
    for tap in range(27):
        u2[tap] = mm_tn(w2_v[tap], q2)
    build_banded(u2, t2, 64, 256, 8, 1, 1)

    sy, sl = iota((256, 512), 0), iota((256, 512), 1)
    split[...] = onehot(sy == 2 * (sl % 128) + sl // 128 - 1)
    ys, js = iota((128, 256), 0), iota((128, 256), 1)
    shift[...] = onehot(ys == jnp.where(js < 128, js - 1, js - 127))

    def stack(i, h, pack, left, right, keep):
        d = mm(x_v[i, pl.ds(h * 16, 16)].reshape(256, 256), split[...])
        r32, l32 = iota((32, 256), 0), iota((32, 256), 1)
        pick = onehot(((r32 == left) & (l32 == 0)) | ((r32 == right) & (l32 == 255)))
        e = mm_tn(pack, pick)
        full = jnp.concatenate([d[:, :128] + e[:, :128], d[:, 128:384], d[:, 384:] + e[:, 128:]], axis=1)
        if keep is not None:
            full = full * keep
        full = full.astype(BF)
        for f in range(3):
            start = pl.multiple_of(i * 1536 + h * 768 + f * 256, 256)
            bb[pl.ds(start, 256), :] = full[:, f * 128:f * 128 + 256]

    fine[(0, 1)].wait_recv()
    fine[(0, -1)].wait_recv()

    def own_row(i, carry):
        left = jnp.where(first_y, -1, 2 * (i - 1) + 1)
        right = jnp.where(last_y, -1, 16 + 2 * (i - 1))
        for h in range(2):
            stack(i, h, fine_pk[0:2, :, h * 256:(h + 1) * 256].reshape(32, 256), left, right, None)
        return carry

    lax.fori_loop(1, 5, own_row, 0)

    acc[0] = mm(t1[:, 1536:], bb[1536:4608, :])
    acc[3] = mm(t1[:, :3072], bb[4608:7680, :])

    def middle(i, carry):
        acc[i] = mm(t1[...], bb[pl.ds(pl.multiple_of(i * 1536, 512), 4608), :])
        return carry

    lax.fori_loop(1, 3, middle, 0)

    q3 = onehot(iota((64, 512), 1) // 8 == iota((64, 512), 0))
    u3[...] = mm(w3_v[...].reshape(1728, 64), q3).reshape(27, 64, 512)
    build_banded(u3, t3, 64, 512, 8, 1, 1)

    r144 = iota((144, 256), 0)
    l144 = iota((144, 256), 1)
    for jj in range(6):
        dx, j = ((-1, 0, 1)[jj // 2], jj % 2)
        left = slot_of(dx, -1) * 16 + j * 4 + 3
        right = slot_of(dx, 1) * 16 + j * 4
        sel[:, jj * 256:(jj + 1) * 256] = onehot(
            ((r144 == left) & (l144 == 0)) | ((r144 == right) & (l144 == 255)))
    re, le = iota((144, 128), 0), iota((144, 128), 1)
    xo, side = le // 2, le % 2
    for a in range(3):
        jj = xo + a
        group = jnp.where(jj < 2, 1, jnp.where(jj < 4, 0, 2))
        for f in range(3):
            dyl, cil = ((1, 2), (1, 3), (0, 0))[f]
            dyr, cir = ((0, 3), (2, 0), (2, 1))[f]
            want = jnp.where(side == 0, dyl * 16 + cil, dyr * 16 + cir) + group * 48 + (jj % 2) * 4
            tile = 1536 + (a * 3 + f) * 128
            sel[:, tile:tile + 128] = onehot((re == want) & (le < 8))

    for d in FINE[2:]:
        fine[d].wait_recv()

    def halo_half(h, carry):
        for i, row, base, r, edge in ((1, 0, 2, 3, first_x), (0, 5, 4, 0, last_x)):
            row_copy(i, h).wait_recv()
            left = jnp.where(first_y, -1, 2 * r + 1)
            right = jnp.where(last_y, -1, 16 + 2 * r)
            pack = fine_pk[base:base + 2, :, pl.ds(pl.multiple_of(h * 256, 256), 256)].reshape(32, 256)
            stack(row, h, pack, left, right, jnp.where(edge, 0.0, 1.0))
        k = pl.multiple_of(h * 768, 256)
        acc[0] += mm(t1[:, pl.ds(k, 768)], bb[pl.ds(k, 768), :])
        acc[3] += mm(t1[:, pl.ds(3072 + k, 768)], bb[pl.ds(7680 + k, 768), :])
        return carry

    lax.fori_loop(0, 2, halo_half, 0)

    def pooled_copy(i, j):
        dst, dx = ((p_right, -1), (p_left, 1))[i]
        return pltpu.make_async_remote_copy(
            src_ref=p_own.at[j], dst_ref=dst.at[j], send_sem=send_p.at[i, j], recv_sem=recv_p.at[i, j],
            device_id=at(dx, 0), device_id_type=MESH)

    for j in range(2):
        m = jnp.maximum(acc[2 * j], acc[2 * j + 1])
        m = jnp.maximum(m[:, :128], m[:, 128:])
        m = jnp.maximum(m[:256], m[256:])
        p_own[j] = jnp.maximum(m + bias1[...], 0.0).astype(BF)
        for i in range(2):
            pooled_copy(i, j).start()

    ends = jnp.zeros((16, 256), F32)
    r16, l16 = iota((16, 128), 0), iota((16, 128), 1)
    for j in range(2):
        pick = onehot((r16 // 4 == j) & (l16 == jnp.where(r16 % 4 < 2, r16 % 4, 124 + r16 % 4)))
        ends = ends + mm_nt(pick, p_own[j])
    own_pk2[...] = ends.astype(BF)
    coarse = {}
    for i, d in enumerate(COARSE):
        back = COARSE.index((-d[0], -d[1]))
        coarse[d] = pltpu.make_async_remote_copy(
            src_ref=own_pk2, dst_ref=coarse_pk.at[slot_of(-d[0], -d[1])], send_sem=send_c.at[i],
            recv_sem=recv_c.at[back], device_id=at(*d), device_id_type=MESH)
        coarse[d].start()
    coarse_pk[0] = ends.astype(BF)

    def known(packs, n):
        rr = iota((n, 256), 0) // 16
        gone_x = ((rr // 3 == 1) & first_x) | ((rr // 3 == 2) & last_x)
        gone_y = ((rr % 3 == 1) & first_y) | ((rr % 3 == 2) & last_y)
        return jnp.where(gone_x | gone_y, 0.0, packs.astype(F32)).astype(BF)

    def place(p, ends, spots):
        g = (mm(p, shift[...]) + ends).astype(BF)
        parts = (g[:, :128], p, g[:, 128:])
        for ref, half in spots:
            for f in range(3):
                ref[f * 256:(f + 1) * 256, half * 128:(half + 1) * 128] = parts[f]

    coarse[(0, 1)].wait_recv()
    coarse[(0, -1)].wait_recv()
    e = mm_tn(known(coarse_pk[0:3].reshape(48, 256), 48), sel[0:48, 512:1024])
    place(p_own[0], e[:, :256], ((p_mid, 0),))
    place(p_own[1], e[:, 256:], ((p_mid, 1),))

    def own_second(m, carry):
        rows = pl.ds(pl.multiple_of(m * 256, 256), 256)
        parts = [mm(t2[rows, a * 768:(a + 1) * 768], p_mid[...]) for a in range(3)]
        s_acc[rows, 0:128] = parts[2][:, :128]
        s_acc[rows, 128:256] = parts[2][:, 128:] + parts[1][:, :128]
        s_acc[rows, 256:384] = parts[1][:, 128:] + parts[0][:, :128]
        s_acc[rows, 384:512] = parts[0][:, 128:]
        return carry

    lax.fori_loop(0, 2, own_second, 0)

    for d in COARSE[2:]:
        coarse[d].wait_recv()
    e = mm_tn(known(coarse_pk[...].reshape(144, 256), 144), sel[...])
    for k in range(9):
        p_edge[k * 256:(k + 1) * 256, :] = e[:, 1536 + k * 128:1664 + k * 128].astype(BF)
    for j in range(2):
        for i, src, base, edge in ((1, p_left, 0, first_x), (0, p_right, 4, last_x)):
            pooled_copy(i, j).wait_recv()
            jj = base + j
            spots = {0: ((p_lo, 0),), 1: ((p_lo, 1), (p_mix, 0)), 4: ((p_mix, 1), (p_hi, 0)), 5: ((p_hi, 1),)}[jj]
            p = (src[j].astype(F32) * jnp.where(edge, 0.0, 1.0)).astype(BF)
            place(p, e[:, jj * 256:(jj + 1) * 256], spots)

    lane = iota((1, 640), 1)
    tile, low = lane // 128, lane % 128
    row = jnp.where(tile < 4, tile, low // 2)
    gone = ((row == 0) & first_x) | ((row == 3) & last_x)
    gone = gone | ((tile == 4) & (((low % 2 == 0) & first_y) | ((low % 2 == 1) & last_y)))
    keep = jnp.where(gone, 0.0, 1.0)

    def second(m, carry):
        rows = pl.ds(pl.multiple_of(m * 256, 256), 256)
        lo = mm(t2[rows, 0:768], p_lo[...])
        mix = mm(t2[rows, 768:1536], p_mix[...])
        hi = mm(t2[rows, 1536:2304], p_hi[...])
        edge = mm(t2[rows, :], p_edge[...])
        added = (lo[:, :128] + mix[:, :128], lo[:, 128:], hi[:, :128], mix[:, 128:] + hi[:, 128:])
        for t in range(5):
            cut = slice(t * 128, (t + 1) * 128)
            total = edge if t == 4 else s_acc[rows, cut] + added[t]
            s_v[rows, cut] = (jnp.maximum(total + bias2[rows, :], 0.0) * keep[:, cut]).astype(BF)
        return carry

    lax.fori_loop(0, 2, second, 0)

    ye, je = iota((128, 256), 0), iota((128, 256), 1)
    for x in range(4):
        mid = s_v[:, x * 128:(x + 1) * 128]
        pick = onehot(((ye == 2 * x) & (je == 0)) | ((ye == 2 * x + 1) & (je == 255)))
        both = jnp.concatenate([mid, s_v[:, 512:640]], axis=1)
        g = mm(both, jnp.concatenate([shift[...], pick], axis=0)).astype(BF)
        parts = (g[:, :128], mid, g[:, 128:])
        for a in range(3):
            if 0 <= x - a < 2:
                for f in range(3):
                    top = (a * 3 + f) * 512
                    s3[top:top + 512, (x - a) * 128:(x - a + 1) * 128] = parts[f]

    def third(m, carry):
        rows = pl.ds(pl.multiple_of(m * 256, 256), 256)
        c = mm(t3[rows, :], s3[...])
        for x in range(2):
            block = jnp.maximum(c[:, x * 128:(x + 1) * 128] + bias3[rows, :], 0.0)
            out[pl.ds(m * 32, 32), x] = block.reshape(32, 8, 128).astype(BF)
        return carry

    lax.fori_loop(0, 2, third, 0)

    for i in range(2):
        for h in range(2):
            row_copy(i, h).wait_send()
            pooled_copy(i, h).wait_send()
    for copy in list(fine.values()) + list(coarse.values()):
        copy.wait_send()


def per_device(image, w_first, b_first, w_second, b_second, w_third, b_third):
    nx, ny = lax.axis_size("gx"), lax.axis_size("gy")
    w1 = jnp.transpose(w_first, (2, 3, 4, 0, 1)).reshape(27, 32, 32)
    w2 = jnp.transpose(w_second, (2, 3, 4, 1, 0)).reshape(27, 32, 64)
    w3 = jnp.transpose(w_third, (2, 3, 4, 0, 1)).reshape(27, 64, 64)
    anywhere = pl.BlockSpec(memory_space=pltpu.HBM)
    dma = pltpu.SemaphoreType.DMA
    return pl.pallas_call(
        functools.partial(kernel, nx, ny),
        out_shape=jax.ShapeDtypeStruct((64, 2, 8, 128), BF),
        in_specs=[anywhere] * 7,
        out_specs=pl.BlockSpec(memory_space=pltpu.VMEM),
        scratch_shapes=[
            pltpu.VMEM((6, 32, 16, 256), BF),
            pltpu.VMEM((27, 32, 32), BF),
            pltpu.VMEM((27, 32, 64), BF),
            pltpu.VMEM((27, 64, 64), BF),
            pltpu.VMEM((27, 32, 512), F32),
            pltpu.VMEM((27, 64, 256), F32),
            pltpu.VMEM((27, 64, 512), F32),
            pltpu.VMEM((512, 4608), BF),
            pltpu.VMEM((512, 2304), BF),
            pltpu.VMEM((512, 4608), BF),
            pltpu.VMEM((9216, 256), BF),
            pltpu.VMEM((4, 512, 256), F32),
            pltpu.VMEM((256, 512), BF),
            pltpu.VMEM((128, 256), BF),
            pltpu.VMEM((6, 16, 512), BF),
            pltpu.VMEM((16, 512), BF),
            pltpu.VMEM((144, 2688), BF),
            pltpu.VMEM((2, 256, 128), BF),
            pltpu.VMEM((2, 256, 128), BF),
            pltpu.VMEM((2, 256, 128), BF),
            pltpu.VMEM((9, 16, 256), BF),
            pltpu.VMEM((16, 256), BF),
            pltpu.VMEM((768, 256), BF),
            pltpu.VMEM((768, 256), BF),
            pltpu.VMEM((768, 256), BF),
            pltpu.VMEM((768, 256), BF),
            pltpu.VMEM((2304, 128), BF),
            pltpu.VMEM((512, 512), F32),
            pltpu.VMEM((512, 640), BF),
            pltpu.VMEM((4608, 256), BF),
            pltpu.VMEM((256, 128), F32),
            pltpu.VMEM((512, 128), F32),
            pltpu.VMEM((512, 128), F32),
            pltpu.SMEM((32,), F32),
            pltpu.SMEM((64,), F32),
            pltpu.SMEM((64,), F32),
            dma((10,)), dma((2, 2)), dma((2, 2)), dma((6,)), dma((6,)),
            dma((2, 2)), dma((2, 2)), dma((8,)), dma((8,)),
        ],
        compiler_params=pltpu.CompilerParams(
            collective_id=0, has_side_effects=True, vmem_limit_bytes=67043328 - 300 * 1024),
        name="encoder",
    )(image, w1, b_first, w2, b_second, w3, b_third)


def solution(mesh):
    placed = (P(None, "gx", None, "gy"), P(), P(), P(), P(), P(), P())
    return jax.shard_map(
        per_device, mesh=mesh, in_specs=placed, out_specs=P(None, "gx", None, "gy"), check_vma=False
    )
```

time: 58.8 us -> 45.5 us (0.77)
  the two profiles are of different devices: /device:TPU:8 before, /device:TPU:32 now
where the time goes in v2:
time: 45.5 us; the launch traced here: 45.4 us
  Pallas kernels  43.7 us (96%)
  local copies, waits for them, and re-layouts  1.67 us (4%)
    pallas_call x1, Pallas kernels, per_device(): pl.pallas_call(functools.partial(kernel, nx, ny), out_shape=jax.ShapeDtyp...  43.7 us
    unnamed x1, local copies, waits for them, and re-layouts  1.67 us

profile of v2, /device:TPU:32, one launch (start us, length us, event | category | flops | bytes accessed | tf_op | source)
XLA Modules:
  0.0 45.4 jit_solution(6402841172719750653)
XLA Ops:
  0.0 43.7 %encoder.1 = bf16[64,2,8,128]{3,2,1,0:T(8,128)(2,1)} custom-call(bf16[32,4,16,256]{3,2,1,0:T(8,128)(2,1)} %image.1, bf16[27,32,32]{2,1,0:T(8,128)(2,1)} %bitcast.10, f32[32]{0:T(128)} %b1.1, bf16[27,32,64]{2,1,0:T(8,128)(2,1)} %bitcast.11, f32[64]{0:T(128)} %b2.1, bf16[27,64,64]{2,1,0:T(8,128)(2,1)} %bitcast.9, f32[64]{0:T(128)} %b3.1), custom_call_target="tpu_custom_call" | custom-call | tf_op jit(solution)/shard_map/encoder/pallas_call | solution.py:353
  43.7 1.7 %copy.9 = bf16[64,2,8,128]{3,2,1,0:T(8,128)(2,1)} copy(bf16[64,2,8,128]{3,2,1,0:T(8,128)(2,1)} %encoder.1) | data formatting | bytes 524288

commit v3 on v2

--- a/solution.py
+++ b/solution.py
@@ -138,6 +138,10 @@
         u2[tap] = mm_tn(w2_v[tap], q2)
     build_banded(u2, t2, 64, 256, 8, 1, 1)
 
+    q3 = onehot(iota((64, 512), 1) // 8 == iota((64, 512), 0))
+    u3[...] = mm(w3_v[...].reshape(1728, 64), q3).reshape(27, 64, 512)
+    build_banded(u3, t3, 64, 512, 8, 1, 1)
+
     sy, sl = iota((256, 512), 0), iota((256, 512), 1)
     split[...] = onehot(sy == 2 * (sl % 128) + sl // 128 - 1)
     ys, js = iota((128, 256), 0), iota((128, 256), 1)
@@ -176,10 +180,6 @@
         return carry
 
     lax.fori_loop(1, 3, middle, 0)
-
-    q3 = onehot(iota((64, 512), 1) // 8 == iota((64, 512), 0))
-    u3[...] = mm(w3_v[...].reshape(1728, 64), q3).reshape(27, 64, 512)
-    build_banded(u3, t3, 64, 512, 8, 1, 1)
 
     r144 = iota((144, 256), 0)
     l144 = iota((144, 256), 1)
@@ -282,6 +282,21 @@
     e = mm_tn(known(coarse_pk[...].reshape(144, 256), 144), sel[...])
     for k in range(9):
         p_edge[k * 256:(k + 1) * 256, :] = e[:, 1536 + k * 128:1664 + k * 128].astype(BF)
+    lane = iota((1, 640), 1)
+    tile, low = lane // 128, lane % 128
+    row = jnp.where(tile < 4, tile, low // 2)
+    gone = ((row == 0) & first_x) | ((row == 3) & last_x)
+    gone = gone | ((tile == 4) & (((low % 2 == 0) & first_y) | ((low % 2 == 1) & last_y)))
+    keep = jnp.where(gone, 0.0, 1.0)
+
+    def edges(m, carry):
+        rows = pl.ds(pl.multiple_of(m * 256, 256), 256)
+        total = mm(t2[rows, :], p_edge[...]) + bias2[rows, :]
+        s_v[rows, 512:640] = (jnp.maximum(total, 0.0) * keep[:, 512:640]).astype(BF)
+        return carry
+
+    lax.fori_loop(0, 2, edges, 0)
+
     for j in range(2):
         for i, src, base, edge in ((1, p_left, 0, first_x), (0, p_right, 4, last_x)):
             pooled_copy(i, j).wait_recv()
@@ -290,23 +305,15 @@
             p = (src[j].astype(F32) * jnp.where(edge, 0.0, 1.0)).astype(BF)
             place(p, e[:, jj * 256:(jj + 1) * 256], spots)
 
-    lane = iota((1, 640), 1)
-    tile, low = lane // 128, lane % 128
-    row = jnp.where(tile < 4, tile, low // 2)
-    gone = ((row == 0) & first_x) | ((row == 3) & last_x)
-    gone = gone | ((tile == 4) & (((low % 2 == 0) & first_y) | ((low % 2 == 1) & last_y)))
-    keep = jnp.where(gone, 0.0, 1.0)
-
     def second(m, carry):
         rows = pl.ds(pl.multiple_of(m * 256, 256), 256)
         lo = mm(t2[rows, 0:768], p_lo[...])
         mix = mm(t2[rows, 768:1536], p_mix[...])
         hi = mm(t2[rows, 1536:2304], p_hi[...])
-        edge = mm(t2[rows, :], p_edge[...])
         added = (lo[:, :128] + mix[:, :128], lo[:, 128:], hi[:, :128], mix[:, 128:] + hi[:, 128:])
-        for t in range(5):
+        for t in range(4):
             cut = slice(t * 128, (t + 1) * 128)
-            total = edge if t == 4 else s_acc[rows, cut] + added[t]
+            total = s_acc[rows, cut] + added[t]
             s_v[rows, cut] = (jnp.maximum(total + bias2[rows, :], 0.0) * keep[:, cut]).astype(BF)
         return carry
 
@@ -396,9 +403,10 @@
             dma((2, 2)), dma((2, 2)), dma((8,)), dma((8,)),
         ],
         compiler_params=pltpu.CompilerParams(
-            collective_id=0, has_side_effects=True, vmem_limit_bytes=67043328 - 300 * 1024),
+            collective_id=0, has_side_effects=True, vmem_limit_bytes=48 * 1024 * 1024),
         name="encoder",
-    )(image, w1, b_first, w2, b_second, w3, b_third)
+    )(*(pltpu.with_memory_space_constraint(v, pltpu.HBM)
+        for v in (image, w1, b_first, w2, b_second, w3, b_third)))
 
 
 def solution(mesh):

time: 45.5 us -> 43.8 us (0.963)
  local copies, waits for them, and re-layouts: 1.67 us -> 0.71 us
  Pallas kernels: 43.7 us -> 43 us
    unnamed x1, local copies, waits for them, and re-layouts: 1.67 us -> 0.71 us
    pallas_call x1, Pallas kernels: 43.7 us -> 43 us  [per_device(): pl.pallas_call(functools.partial(kernel, nx, ny), out_shape=jax.ShapeDtyp...]
where the time goes in v3:
time: 43.8 us; the launch traced here: 43.7 us
  Pallas kernels  43 us (98%)
  local copies, waits for them, and re-layouts  0.71 us (2%)
    pallas_call x1, Pallas kernels, per_device(): pl.pallas_call(functools.partial(kernel, nx, ny), out_shape=jax.ShapeDtyp...  43 us

profile of v3, /device:TPU:32, one launch (start us, length us, event | category | flops | bytes accessed | tf_op | source)
XLA Modules:
  0.0 43.7 jit_solution(9072605601356187103)
XLA Ops:
  0.0 43.0 %encoder.1 = bf16[64,2,8,128]{3,2,1,0:T(8,128)(2,1)S(1)} custom-call(bf16[32,4,16,256]{3,2,1,0:T(8,128)(2,1)} %image.1, bf16[27,32,32]{2,1,0:T(8,128)(2,1)} %bitcast.10, f32[32]{0:T(128)} %b1.1, bf16[27,32,64]{2,1,0:T(8,128)(2,1)} %bitcast.11, f32[64]{0:T(128)} %b2.1, bf16[27,64,64]{2,1,0:T(8,128)(2,1)} %bitcast.9, f32[64]{0:T(128)} %b3.1), custom_call_target="tpu_custom_call" | custom-call | tf_op jit(solution)/shard_map/encoder/pallas_call | solution.py:360
  43.0 0.7 %copy.9 = bf16[64,2,8,128]{3,2,1,0:T(8,128)(2,1)} copy(bf16[64,2,8,128]{3,2,1,0:T(8,128)(2,1)S(1)} %encoder.1) | data formatting | bytes 524288

commit v4 on v3

--- a/solution.py
+++ b/solution.py
@@ -99,8 +99,8 @@
 
     for load in loads[1:5]:
         load.wait()
-    ends = jnp.zeros((16, 512), F32)
-    r16, l16 = iota((16, 256), 0), iota((16, 256), 1)
+    ends = jnp.zeros((8, 512), F32)
+    r16, l16 = iota((8, 256), 0), iota((8, 256), 1)
     for r in range(4):
         pick = onehot(((r16 == 2 * r) & (l16 == 0)) | ((r16 == 2 * r + 1) & (l16 == 255)))
         ends = ends + mm_nt(pick, x_v[r + 1].reshape(512, 256))
@@ -149,9 +149,9 @@
 
     def stack(i, h, pack, left, right, keep):
         d = mm(x_v[i, pl.ds(h * 16, 16)].reshape(256, 256), split[...])
-        r32, l32 = iota((32, 256), 0), iota((32, 256), 1)
+        r32, l32 = iota((16, 256), 0), iota((16, 256), 1)
         pick = onehot(((r32 == left) & (l32 == 0)) | ((r32 == right) & (l32 == 255)))
-        e = mm_tn(pack, pick)
+        e = mm_tn(pack.astype(F32).reshape(16, 256).astype(BF), pick)
         full = jnp.concatenate([d[:, :128] + e[:, :128], d[:, 128:384], d[:, 384:] + e[:, 128:]], axis=1)
         if keep is not None:
             full = full * keep
@@ -165,9 +165,9 @@
 
     def own_row(i, carry):
         left = jnp.where(first_y, -1, 2 * (i - 1) + 1)
-        right = jnp.where(last_y, -1, 16 + 2 * (i - 1))
+        right = jnp.where(last_y, -1, 8 + 2 * (i - 1))
         for h in range(2):
-            stack(i, h, fine_pk[0:2, :, h * 256:(h + 1) * 256].reshape(32, 256), left, right, None)
+            stack(i, h, fine_pk[0:2, :, h * 256:(h + 1) * 256], left, right, None)
         return carry
 
     lax.fori_loop(1, 5, own_row, 0)
@@ -181,15 +181,15 @@
 
     lax.fori_loop(1, 3, middle, 0)
 
-    r144 = iota((144, 256), 0)
-    l144 = iota((144, 256), 1)
+    r144 = iota((72, 256), 0)
+    l144 = iota((72, 256), 1)
     for jj in range(6):
         dx, j = ((-1, 0, 1)[jj // 2], jj % 2)
-        left = slot_of(dx, -1) * 16 + j * 4 + 3
-        right = slot_of(dx, 1) * 16 + j * 4
+        left = slot_of(dx, -1) * 8 + j * 4 + 3
+        right = slot_of(dx, 1) * 8 + j * 4
         sel[:, jj * 256:(jj + 1) * 256] = onehot(
             ((r144 == left) & (l144 == 0)) | ((r144 == right) & (l144 == 255)))
-    re, le = iota((144, 128), 0), iota((144, 128), 1)
+    re, le = iota((72, 128), 0), iota((72, 128), 1)
     xo, side = le // 2, le % 2
     for a in range(3):
         jj = xo + a
@@ -197,7 +197,7 @@
         for f in range(3):
             dyl, cil = ((1, 2), (1, 3), (0, 0))[f]
             dyr, cir = ((0, 3), (2, 0), (2, 1))[f]
-            want = jnp.where(side == 0, dyl * 16 + cil, dyr * 16 + cir) + group * 48 + (jj % 2) * 4
+            want = jnp.where(side == 0, dyl * 8 + cil, dyr * 8 + cir) + group * 24 + (jj % 2) * 4
             tile = 1536 + (a * 3 + f) * 128
             sel[:, tile:tile + 128] = onehot((re == want) & (le < 8))
 
@@ -208,8 +208,8 @@
         for i, row, base, r, edge in ((1, 0, 2, 3, first_x), (0, 5, 4, 0, last_x)):
             row_copy(i, h).wait_recv()
             left = jnp.where(first_y, -1, 2 * r + 1)
-            right = jnp.where(last_y, -1, 16 + 2 * r)
-            pack = fine_pk[base:base + 2, :, pl.ds(pl.multiple_of(h * 256, 256), 256)].reshape(32, 256)
+            right = jnp.where(last_y, -1, 8 + 2 * r)
+            pack = fine_pk[base:base + 2, :, pl.ds(pl.multiple_of(h * 256, 256), 256)]
             stack(row, h, pack, left, right, jnp.where(edge, 0.0, 1.0))
         k = pl.multiple_of(h * 768, 256)
         acc[0] += mm(t1[:, pl.ds(k, 768)], bb[pl.ds(k, 768), :])
@@ -229,11 +229,9 @@
         m = jnp.maximum(m[:, :128], m[:, 128:])
         m = jnp.maximum(m[:256], m[256:])
         p_own[j] = jnp.maximum(m + bias1[...], 0.0).astype(BF)
-        for i in range(2):
-            pooled_copy(i, j).start()
-
-    ends = jnp.zeros((16, 256), F32)
-    r16, l16 = iota((16, 128), 0), iota((16, 128), 1)
+
+    ends = jnp.zeros((8, 256), F32)
+    r16, l16 = iota((8, 128), 0), iota((8, 128), 1)
     for j in range(2):
         pick = onehot((r16 // 4 == j) & (l16 == jnp.where(r16 % 4 < 2, r16 % 4, 124 + r16 % 4)))
         ends = ends + mm_nt(pick, p_own[j])
@@ -245,13 +243,16 @@
             src_ref=own_pk2, dst_ref=coarse_pk.at[slot_of(-d[0], -d[1])], send_sem=send_c.at[i],
             recv_sem=recv_c.at[back], device_id=at(*d), device_id_type=MESH)
         coarse[d].start()
+    for j in range(2):
+        for i in range(2):
+            pooled_copy(i, j).start()
     coarse_pk[0] = ends.astype(BF)
 
     def known(packs, n):
-        rr = iota((n, 256), 0) // 16
+        rr = iota((n, 256), 0) // 8
         gone_x = ((rr // 3 == 1) & first_x) | ((rr // 3 == 2) & last_x)
         gone_y = ((rr % 3 == 1) & first_y) | ((rr % 3 == 2) & last_y)
-        return jnp.where(gone_x | gone_y, 0.0, packs.astype(F32)).astype(BF)
+        return jnp.where(gone_x | gone_y, 0.0, packs.astype(F32).reshape(n, 256)).astype(BF)
 
     def place(p, ends, spots):
         g = (mm(p, shift[...]) + ends).astype(BF)
@@ -262,7 +263,7 @@
 
     coarse[(0, 1)].wait_recv()
     coarse[(0, -1)].wait_recv()
-    e = mm_tn(known(coarse_pk[0:3].reshape(48, 256), 48), sel[0:48, 512:1024])
+    e = mm_tn(known(coarse_pk[0:3], 24), sel[0:24, 512:1024])
     place(p_own[0], e[:, :256], ((p_mid, 0),))
     place(p_own[1], e[:, 256:], ((p_mid, 1),))
 
@@ -279,7 +280,7 @@
 
     for d in COARSE[2:]:
         coarse[d].wait_recv()
-    e = mm_tn(known(coarse_pk[...].reshape(144, 256), 144), sel[...])
+    e = mm_tn(known(coarse_pk[...], 72), sel[...])
     for k in range(9):
         p_edge[k * 256:(k + 1) * 256, :] = e[:, 1536 + k * 128:1664 + k * 128].astype(BF)
     lane = iota((1, 640), 1)
@@ -377,14 +378,14 @@
             pltpu.VMEM((4, 512, 256), F32),
             pltpu.VMEM((256, 512), BF),
             pltpu.VMEM((128, 256), BF),
-            pltpu.VMEM((6, 16, 512), BF),
-            pltpu.VMEM((16, 512), BF),
-            pltpu.VMEM((144, 2688), BF),
+            pltpu.VMEM((6, 8, 512), BF),
+            pltpu.VMEM((8, 512), BF),
+            pltpu.VMEM((72, 2688), BF),
             pltpu.VMEM((2, 256, 128), BF),
             pltpu.VMEM((2, 256, 128), BF),
             pltpu.VMEM((2, 256, 128), BF),
-            pltpu.VMEM((9, 16, 256), BF),
-            pltpu.VMEM((16, 256), BF),
+            pltpu.VMEM((9, 8, 256), BF),
+            pltpu.VMEM((8, 256), BF),
             pltpu.VMEM((768, 256), BF),
             pltpu.VMEM((768, 256), BF),
             pltpu.VMEM((768, 256), BF),

time: 43.8 us -> 41.1 us (0.938)
  Pallas kernels: 43 us -> 40.3 us
    pallas_call x1, Pallas kernels: 43 us -> 40.3 us  [per_device(): pl.pallas_call(functools.partial(kernel, nx, ny), out_shape=jax.ShapeDtyp...]
where the time goes in v4:
time: 41.1 us; the launch traced here: 41 us
  Pallas kernels  40.3 us (98%)
  local copies, waits for them, and re-layouts  0.71 us (2%)
    pallas_call x1, Pallas kernels, per_device(): pl.pallas_call(functools.partial(kernel, nx, ny), out_shape=jax.ShapeDtyp...  40.3 us

profile of v4, /device:TPU:32, one launch (start us, length us, event | category | flops | bytes accessed | tf_op | source)
XLA Modules:
  0.0 41.0 jit_solution(17419598768715439390)
XLA Ops:
  0.0 40.3 %encoder.1 = bf16[64,2,8,128]{3,2,1,0:T(8,128)(2,1)S(1)} custom-call(bf16[32,4,16,256]{3,2,1,0:T(8,128)(2,1)} %image.1, bf16[27,32,32]{2,1,0:T(8,128)(2,1)} %bitcast.10, f32[32]{0:T(128)} %b1.1, bf16[27,32,64]{2,1,0:T(8,128)(2,1)} %bitcast.11, f32[64]{0:T(128)} %b2.1, bf16[27,64,64]{2,1,0:T(8,128)(2,1)} %bitcast.9, f32[64]{0:T(128)} %b3.1), custom_call_target="tpu_custom_call" | custom-call | tf_op jit(solution)/shard_map/encoder/pallas_call | solution.py:361
  40.3 0.7 %copy.9 = bf16[64,2,8,128]{3,2,1,0:T(8,128)(2,1)} copy(bf16[64,2,8,128]{3,2,1,0:T(8,128)(2,1)S(1)} %encoder.1) | data formatting | bytes 524288

commit v5 on v4

--- a/solution.py
+++ b/solution.py
@@ -280,9 +280,10 @@
 
     for d in COARSE[2:]:
         coarse[d].wait_recv()
-    e = mm_tn(known(coarse_pk[...], 72), sel[...])
+    packs = known(coarse_pk[...], 72)
+    e = mm_tn(packs, sel[:, 1536:])
     for k in range(9):
-        p_edge[k * 256:(k + 1) * 256, :] = e[:, 1536 + k * 128:1664 + k * 128].astype(BF)
+        p_edge[k * 256:(k + 1) * 256, :] = e[:, k * 128:(k + 1) * 128].astype(BF)
     lane = iota((1, 640), 1)
     tile, low = lane // 128, lane % 128
     row = jnp.where(tile < 4, tile, low // 2)
@@ -304,7 +305,7 @@
             jj = base + j
             spots = {0: ((p_lo, 0),), 1: ((p_lo, 1), (p_mix, 0)), 4: ((p_mix, 1), (p_hi, 0)), 5: ((p_hi, 1),)}[jj]
             p = (src[j].astype(F32) * jnp.where(edge, 0.0, 1.0)).astype(BF)
-            place(p, e[:, jj * 256:(jj + 1) * 256], spots)
+            place(p, mm_tn(packs, sel[:, jj * 256:(jj + 1) * 256]), spots)
 
     def second(m, carry):
         rows = pl.ds(pl.multiple_of(m * 256, 256), 256)

time: 41.1 us -> 41.3 us (level)
  no operation moved by 1% of the time
where the time goes in v5:
time: 41.3 us; the launch traced here: 41.2 us
  Pallas kernels  40.5 us (98%)
  local copies, waits for them, and re-layouts  0.71 us (2%)
    pallas_call x1, Pallas kernels, per_device(): pl.pallas_call(functools.partial(kernel, nx, ny), out_shape=jax.ShapeDtyp...  40.5 us

profile of v5, /device:TPU:32, one launch (start us, length us, event | category | flops | bytes accessed | tf_op | source)
XLA Modules:
  0.0 41.2 jit_solution(1963696747922519824)
XLA Ops:
  0.0 40.5 %encoder.1 = bf16[64,2,8,128]{3,2,1,0:T(8,128)(2,1)S(1)} custom-call(bf16[32,4,16,256]{3,2,1,0:T(8,128)(2,1)} %image.1, bf16[27,32,32]{2,1,0:T(8,128)(2,1)} %bitcast.10, f32[32]{0:T(128)} %b1.1, bf16[27,32,64]{2,1,0:T(8,128)(2,1)} %bitcast.11, f32[64]{0:T(128)} %b2.1, bf16[27,64,64]{2,1,0:T(8,128)(2,1)} %bitcast.9, f32[64]{0:T(128)} %b3.1), custom_call_target="tpu_custom_call" | custom-call | tf_op jit(solution)/shard_map/encoder/pallas_call | solution.py:362
  40.5 0.7 %copy.9 = bf16[64,2,8,128]{3,2,1,0:T(8,128)(2,1)} copy(bf16[64,2,8,128]{3,2,1,0:T(8,128)(2,1)S(1)} %encoder.1) | data formatting | bytes 524288
